TPU v7x, 256 devices: a whole 4x4x8 slice. The times are simulated.
256 devices in a mesh: contacts: 32 (over y, z), tm: 8 (over x, core).
Axes of the slice: x: 4, y: 4, z: 8, core: 2. Of those that a mesh axis runs over, the one named last changes fastest.
Arguments:
- signal: bfloat16 [8192, 1024], P('contacts', 'tm'), may hold values from -6 to 6
- pos_idx: int32 [8192], P('contacts'), may hold values from 0 to 4095
- live_count: int32 [32], P('contacts'), may hold values from 128 to 256, as said below
- latents: bfloat16 [256, 512], replicated, may hold values from -400 to 400
- pos_table: bfloat16 [4096, 512], replicated, may hold values from -6 to 6
- w_in: bfloat16 [32, 512], replicated, may hold values from -1 to 1
- w_kv: bfloat16 [512, 1024], replicated, may hold values from -0.25 to 0.25
- w_query: bfloat16 [512, 512], replicated, may hold values from -0.25 to 0.25
- w_out: bfloat16 [512, 512], replicated, may hold values from -0.25 to 0.25
- conv_weight: bfloat16 [2, 3, 512, 512], replicated, may hold values from -0.15625 to 0.15625
- conv_bias: float32 [2, 512], replicated, may hold values from -3 to 3
- cotangent: bfloat16 [32, 256, 512], P('tm', 'contacts'), may hold values from -6 to 6
Outputs:
- features: bfloat16 [32, 256, 512], P('tm', 'contacts')
- d_latents: float32 [256, 512], replicated
Inputs may be any that keep to these rules, and one draw needn't show every extreme that they name: The first live_count[b] contacts of block b are valid; some block is full and some block has exactly 128 valid contacts.
All inputs are finite; a program needn't handle non-finite values.
Results may differ from a plain program's by a relative error of at most 0.018.
The roundings to bfloat16 on the way count: a program that leaves them out, or rounds other values in their place, can miss the bound.
Values may be sent and summed in bfloat16 or wider, within the bound.
No kernel may reach another device: no remote copies, remote signals or barrier semaphores. Data moves between devices by JAX's collectives and lax.ppermute only.
A program may use at most 192 MiB of HBM per device.

v0:
```python
import jax
import jax.numpy as jnp
from jax import lax
from jax.sharding import PartitionSpec as P

HD = 64
PATCH = 32
KSIZE = 3
LAYERS = 2
neg_big = -1e30
scale_dot = 0.125


def joined(x, axis, combine):
    everything = jax.tree.map(lambda part: lax.all_gather(part, axis), x)
    first = jax.tree.map(lambda part: part[0], everything)

    def step(k, so_far):
        return combine(so_far, jax.tree.map(lambda part: part[k], everything))

    return lax.fori_loop(1, lax.axis_size(axis), step, first)


def with_halo(x, sides, width):
    for axis, dim in sides:
        peers, length = (lax.axis_size(axis), x.shape[dim])
        up = [(i, (i + 1) % peers) for i in range(peers - 1)]
        down = [(j, i) for i, j in up]
        last = lax.slice_in_dim(x, length - width, length, axis=dim)
        first = lax.slice_in_dim(x, 0, width, axis=dim)
        before = lax.ppermute(last, axis, up)
        after = lax.ppermute(first, axis, down)
        x = jnp.concatenate([before, x, after], axis=dim)
    return x


def silu_slope(pre_act):
    sigmoid_v = jax.nn.sigmoid(pre_act)
    return sigmoid_v * (1.0 + pre_act * (1.0 - sigmoid_v))


def split_heads(values, head_count):
    return values.reshape(values.shape[:-1] + (head_count, values.shape[-1] // head_count))


def combine_parts(part_a, part_b):
    top_a, sum_a, acc_a = part_a
    top_b, sum_b, acc_b = part_b
    top_score = jnp.maximum(top_a, top_b)
    fac_a = jnp.exp(top_a - top_score)
    fac_b = jnp.exp(top_b - top_score)
    head_count = top_score.shape[-1]
    merged = (
        split_heads(acc_a, head_count) * fac_a[..., None]
        + split_heads(acc_b, head_count) * fac_b[..., None]
    )
    return (top_score, sum_a * fac_a + sum_b * fac_b, merged.reshape(acc_a.shape))


def normalize(accum_out, totals):
    head_count = totals.shape[-1]
    return (
        (split_heads(accum_out, head_count) / totals[..., None])
        .reshape(accum_out.shape)
        .astype(jnp.bfloat16)
    )


def conv_apply(source, weight, bias_row, dilation, out_count):
    stacked = jnp.stack(
        [source[j * dilation : j * dilation + out_count] for j in range(KSIZE)], axis=2
    )
    return (
        jnp.einsum("tlji,jio->tlo", stacked, weight, preferred_element_type=jnp.float32) + bias_row
    )


def local(
    signal,
    pos_idx,
    live_count,
    latents,
    pos_table,
    w_in,
    w_kv,
    w_query,
    w_out,
    conv_weight,
    conv_bias,
    cotangent,
):
    con_dev = signal.shape[0]
    pat_dev = signal.shape[1] // PATCH
    model_width = w_query.shape[0]
    head_count = model_width // HD
    lat_rows = latents.shape[0]
    groups = lax.axis_size("contacts")
    lat_dev = lat_rows // groups
    owner_idx = lax.axis_index("contacts")
    is_valid = jnp.arange(con_dev, dtype=jnp.int32) < live_count[0]
    embedded = jnp.einsum(
        "cpt,td->pcd",
        signal.reshape(con_dev, pat_dev, PATCH),
        w_in,
        preferred_element_type=jnp.float32,
    )
    pos_rows = jnp.take(pos_table, pos_idx, axis=0).astype(jnp.float32)
    tokens = (embedded + pos_rows[None]).astype(jnp.bfloat16)
    keyval = jnp.dot(
        tokens.reshape(pat_dev * con_dev, model_width), w_kv, preferred_element_type=jnp.float32
    ).astype(jnp.bfloat16)
    keyval = keyval.reshape(pat_dev // 2, 2, con_dev, 2, head_count, HD)
    queries = (
        jnp.dot(latents, w_query, preferred_element_type=jnp.float32)
        .astype(jnp.bfloat16)
        .reshape(lat_rows, head_count, HD)
    )

    def masked_scores(key_block):
        scores = (
            jnp.einsum("ihe,pche->phic", queries, key_block, preferred_element_type=jnp.float32)
            * scale_dot
        )
        return jnp.where(is_valid, scores, neg_big)

    def attend(kv_block):
        scores = masked_scores(kv_block[:, :, 0])
        top_score = jnp.max(scores, axis=3)
        weights = jnp.where(is_valid, jnp.exp(scores - top_score[..., None]), 0.0)
        totals = jnp.sum(weights, axis=3)
        accum_out = jnp.einsum(
            "phic,pche->pihe",
            weights.astype(jnp.bfloat16),
            kv_block[:, :, 1],
            preferred_element_type=jnp.float32,
        )
        return (
            jnp.swapaxes(top_score, 1, 2),
            jnp.swapaxes(totals, 1, 2),
            accum_out.reshape(2, lat_rows, model_width),
        )

    top_score, totals, accum_out = lax.map(attend, keyval)
    top_score = top_score.reshape(pat_dev, lat_rows, head_count)
    totals = totals.reshape(pat_dev, lat_rows, head_count)
    accum_out = accum_out.reshape(pat_dev, lat_rows, model_width)
    top_all, total_all, acc_all = joined((top_score, totals, accum_out), "contacts", combine_parts)
    attended_all = normalize(acc_all, total_all)
    attended = lax.dynamic_slice_in_dim(attended_all, owner_idx * lat_dev, lat_dev, 1)
    start_x = (
        jnp.dot(
            attended.reshape(pat_dev * lat_dev, model_width),
            w_out,
            preferred_element_type=jnp.float32,
        )
        .astype(jnp.bfloat16)
        .reshape(pat_dev, lat_dev, model_width)
    )
    hidden_list = []
    current = start_x
    for layer_no in range(LAYERS):
        dilation = 2**layer_no
        padded = with_halo(current, (("tm", 0),), dilation * (KSIZE // 2))
        pre_act = conv_apply(padded, conv_weight[layer_no], conv_bias[layer_no], dilation, pat_dev)
        current = (current.astype(jnp.float32) + jax.nn.silu(pre_act)).astype(jnp.bfloat16)
        hidden_list.append(pre_act)
    grad_now = cotangent.astype(jnp.float32)
    for layer_no in reversed(range(LAYERS)):
        dilation = 2**layer_no
        grad_pre = (grad_now * silu_slope(hidden_list[layer_no])).astype(jnp.bfloat16)
        padded = with_halo(grad_pre, (("tm", 0),), dilation * (KSIZE // 2))
        stacked = jnp.stack(
            [
                padded[(KSIZE - 1 - j) * dilation : (KSIZE - 1 - j) * dilation + pat_dev]
                for j in range(KSIZE)
            ],
            axis=2,
        )
        grad_now = grad_now + jnp.einsum(
            "tljo,jio->tli", stacked, conv_weight[layer_no], preferred_element_type=jnp.float32
        )
    grad_att = lax.dot_general(
        grad_now.astype(jnp.bfloat16).reshape(pat_dev * lat_dev, model_width),
        w_out,
        (((1,), (1,)), ((), ())),
        preferred_element_type=jnp.float32,
    )
    grad_att = grad_att.astype(jnp.bfloat16).reshape(pat_dev, lat_dev, model_width)
    grad_all = lax.all_gather(grad_att, "contacts", axis=1, tiled=True)
    delta_row = jnp.sum(
        split_heads(grad_all.astype(jnp.float32), head_count)
        * split_heads(attended_all.astype(jnp.float32), head_count),
        axis=3,
    )

    def back_block(dq_sum, parts):
        kv_block, grad_block, top_block, total_block, delta_block = parts
        key_block = kv_block[:, :, 0]
        scores = masked_scores(key_block)
        top_now = jnp.swapaxes(top_block, 1, 2)
        total_now = jnp.swapaxes(total_block, 1, 2)
        prob_vals = jnp.where(
            is_valid, jnp.exp(scores - top_now[..., None]) / total_now[..., None], 0.0
        )
        grad_prob = jnp.einsum(
            "pihe,pche->phic",
            split_heads(grad_block, head_count),
            kv_block[:, :, 1],
            preferred_element_type=jnp.float32,
        )
        delta_now = jnp.swapaxes(delta_block, 1, 2)
        dscore = (prob_vals * (grad_prob - delta_now[..., None])).astype(jnp.bfloat16)
        return (
            dq_sum
            + jnp.einsum("phic,pche->ihe", dscore, key_block, preferred_element_type=jnp.float32),
            None,
        )

    pairs = pat_dev // 2
    dq_sum, unused = lax.scan(
        back_block,
        jnp.zeros((lat_rows, head_count, HD), jnp.float32),
        (
            keyval,
            grad_all.reshape(pairs, 2, lat_rows, model_width),
            top_all.reshape(pairs, 2, lat_rows, head_count),
            total_all.reshape(pairs, 2, lat_rows, head_count),
            delta_row.reshape(pairs, 2, lat_rows, head_count),
        ),
    )
    query_grad = lax.psum((dq_sum * scale_dot).reshape(lat_rows, model_width), ("contacts", "tm"))
    d_latents = lax.dot_general(
        query_grad.astype(jnp.bfloat16),
        w_query,
        (((1,), (1,)), ((), ())),
        preferred_element_type=jnp.float32,
    )
    return (current, d_latents)


def solution(mesh):
    in_specs = (
        P("contacts", "tm"),
        P("contacts"),
        P("contacts"),
        P(),
        P(),
        P(),
        P(),
        P(),
        P(),
        P(),
        P(),
        P("tm", "contacts", None),
    )
    out_specs = (P("tm", "contacts", None), P())
    return jax.shard_map(local, mesh=mesh, in_specs=in_specs, out_specs=out_specs, check_vma=False)
```

profile of v0, /device:TPU:1, one launch (start us, length us, event | category | flops | bytes accessed | tf_op | source)
XLA Modules:
  0.0 1136.9 jit_solution(8328710909862078384)
XLA Ops:
  9.6 3.9 gather_fusion
  15.5 4.0 reshape.142
  19.5 5.5 copy.76
  25.4 12.2 %while.46 = (s32[]{:T(128)}, f32[2,2,256,8]{2,3,1,0:T(8,128)S(1)}, f32[2,2,256,8]{2,3,1,0:T(8,128)S(1)}, f32[2,2,256,512]{3,2,1,0:T(8,128)}, bf16[2,2,256,2,8,64...) while((s32[]{:T(128)}, f32[2,2,256,8]{2,3,1,0:T(8,128)S(1)}, ...), condition=%wide.region_3.4_spmd.clone, body=%wide.region_0.3_spmd.clone.sunk | while | flops 277864704 | bytes 21349984 | solution.py:143
  39.8 73.7 %all-gather.7.cloned.1.call-done = f32[32,4,256,8]{2,3,1,0:T(8,128)} async-done(((f32[1,4,256,8]{2,3,1,0:T(8,128)}), f32[32,4,256,8]{2,3,1,0:T(8,128)}) %all-gather.7.cloned.1.call-update) | async-done | bytes 1048592 | tf_op jit(solution)/shard_map/all_gather | solution.py:15
  114.2 76.3 %all-gather.5.cloned.1.call-done = f32[32,4,256,8]{2,3,1,0:T(8,128)} async-done(((f32[1,4,256,8]{2,3,1,0:T(8,128)}), f32[32,4,256,8]{2,3,1,0:T(8,128)}) %all-gather.5.cloned.1.call-update) | async-done | bytes 1048592 | tf_op jit(solution)/shard_map/all_gather | solution.py:15
  191.3 434.8 %all-gather.9.cloned.1.call-done = f32[32,4,256,512]{3,2,1,0:T(8,128)} async-done(((f32[1,4,256,512]{3,2,1,0:T(8,128)}), f32[32,4,256,512]{3,2,1,0:T(8,128)}) %all-gather.9.cloned.1.call-update) | async-done | bytes 67108880 | tf_op jit(solution)/shard_map/all_gather | solution.py:15
  629.7 282.2 %while.45 = (s32[]{:T(128)}, f32[4,256,8]{1,2,0:T(8,128)S(1)}, f32[4,256,8]{1,2,0:T(8,128)S(1)}, f32[4,256,512]{1,2,0:T(8,128)}, f32[32,4,256,8]{2,3,1,0:T(8,128...) while((s32[]{:T(128)}, f32[4,256,8]{1,2,0:T(8,128)S(1)}, ...), condition=%wide.region_5.6_spmd, body=%wide.region_4.5_spmd.sunk | while | flops 1622021 | bytes 15007895 | solution.py:21
  635.5 3.2 fusion.147
  644.6 3.2 fusion.147
  653.7 3.2 fusion.147
  662.8 3.2 fusion.147
  671.9 3.2 fusion.147
  681.1 3.2 fusion.147
  690.2 3.2 fusion.147
  863.1 3.2 fusion.147
  914.3 4.5 collective-permute-start
  935.6 3.6 collective-permute-start.5
  942.6 4.4 collective-permute-start.7
  950.5 69.0 %all-gather.11.cloned.1.call-done = bf16[4,256,512]{2,0,1:T(4,128)(2,1)} async-done(((bf16[4,8,512]{2,0,1:T(4,128)(2,1)}), bf16[4,256,512]{2,0,1:T(4,128)(2,1)}) %all-gather.11.cloned.1.call-update) | async-done | bytes 1048592 | tf_op jit(solution)/shard_map/all_gather | solution.py:189
  1022.1 23.4 %while.47 = (s32[]{:T(128)}, f32[256,8,64]{0,2,1:T(8,128)}, bf16[2,2,256,2,8,64]{2,5,1,4,3,0:T(8,128)(2,1)}, bf16[256,8,64]{0,2,1:T(8,128)(2,1)S(1)}, f32[2,2,25...) while((s32[]{:T(128)}, f32[256,8,64]{0,2,1:T(8,128)}, ...), condition=%wide.region_8.9_spmd.clone, body=%wide.region_7.8_spmd.clone.sunk | while | flops 411304192 | bytes 15189387 | solution.py:220
  1028.5 5.3 fusion.155
  1040.1 5.5 fusion.155
  1046.7 82.5 %all-reduce.1 = bf16[256,512]{0,1:T(8,128)(2,1)S(1)} all-reduce(f32[256,512]{0,1:T(8,128)S(1)} %bitcast.319), channel_id=1, replica_groups=mesh['contacts'=32,'tm'=8] {'contacts','tm'}, use_global_device_ids=true, to_apply=%region_9.10 | all-reduce | flops 131072 | bytes 786432 | tf_op jit(solution)/shard_map/psum | solution.py:231
  (232 shorter events, 323.4 us)
Async XLA Ops:
  7.2 7.0 copy-start
  7.2 6.5 copy-start.6
  7.2 106.3 %all-gather.7.cloned.1.call-start = ((), (), s32[]{:S(2)}) async-start(), calls=%async_computation.1 | async-start | bytes 1081344 | tf_op jit(solution)/shard_map/all_gather | solution.py:15
  19.4 5.5 copy-start.1
  19.4 5.5 copy-start.5
  37.6 0.6 copy-start.8
  37.6 0.7 copy-start.7
  38.2 152.3 %all-gather.5.cloned.1.call-start = ((), (), s32[]{:S(2)}) async-start(), calls=%async_computation | async-start | bytes 1081344 | tf_op jit(solution)/shard_map/all_gather | solution.py:15
  39.0 587.1 %all-gather.9.cloned.1.call-start = ((), (), s32[]{:S(2)}) async-start(), calls=%async_computation.2 | async-start | bytes 69206016 | tf_op jit(solution)/shard_map/all_gather | solution.py:15
  39.7 979.8 %all-gather.11.cloned.1.call-start = ((), (), s32[]{:S(2)}) async-start(), calls=%async_computation.3 | async-start | bytes 1081344 | tf_op jit(solution)/shard_map/all_gather | solution.py:189
  911.9 2.2 copy-start.3
  911.9 8.9 copy-start.9
  914.1 18.5 %copy-start.4 = (bf16[2,3,512,512]{3,2,1,0:T(8,128)(2,1)S(1)}, bf16[2,3,512,512]{3,2,1,0:T(8,128)(2,1)}, u32[]{:S(2)}) copy-start(bf16[2,3,512,512]{3,2,1,0:T(8,128)(2,1)} %param.27) | copy-start | bytes 9437188
  914.1 18.6 %copy-start.10 = (bf16[4,8,512]{2,1,0:T(8,128)(2,1)S(1)}, bf16[4,8,512]{2,1,0:T(8,128)(2,1)}, u32[]{:S(2)}) copy-start(bf16[4,8,512]{2,1,0:T(8,128)(2,1)} %param.29) | copy-start | bytes 98308
  914.3 6.5 collective-permute-start
  918.9 5.0 collective-permute-start.1
  925.7 4.3 collective-permute-start.2
  927.6 5.1 collective-permute-start.3
  933.7 5.6 collective-permute-start.4
  935.6 4.5 collective-permute-start.5
  940.7 6.3 collective-permute-start.6
  942.6 5.0 collective-permute-start.7
  1045.6 83.6 %copy-start.2 = (bf16[512,512]{1,0:T(8,128)(2,1)S(1)}, bf16[512,512]{1,0:T(8,128)(2,1)}, u32[]{:S(2)}) copy-start(bf16[512,512]{1,0:T(8,128)(2,1)} %param.25) | copy-start | bytes 1572868
Sparse Core Ops, SparseCore 0:
  38.4 75.0 all-gather.6
  116.6 73.8 all-gather.4
  193.1 432.8 all-gather.8
  950.6 68.8 all-gather.10
where the time goes:
time: 1140 us
  waiting for transfers between devices  662 us (58%)
  local copies, waits for them, and re-layouts  191 us (17%)
  other arithmetic  136 us (12%)
  blocking collectives  82.5 us (7%)
  matrix products  28.2 us (2%)
  starting transfers between devices  22.8 us (2%)
  between operations  14.1 us (1%)
    all_gather x3, waiting for transfers between devices, joined(): everything = jax.tree.map(lambda part: lax.all_gather(part, axis), x)  585 us
    dynamic_slice x62, local copies, waits for them, and re-layouts, step(): return combine(so_far, jax.tree.map(lambda part: part[k], everything))  156 us
    add x31, other arithmetic, combine_parts(): split_heads(acc_a, head_count) * fac_a[..., None]  100 us
    psum x1, blocking collectives, local(): lax.psum((dq_sum * scale_dot).reshape(lat_rows, model_width), ('contacts'...  82.5 us
    all_gather x1, waiting for transfers between devices, local(): grad_all = lax.all_gather(grad_att, 'contacts', axis=1, tiled=True)  69 us
    add x31, other arithmetic, combine_parts(): sum_a * fac_a + sum_b * fac_b  25.1 us
  transfers between devices with their start and end apart: 12, of which 8 were waited for; matrix products, arithmetic and copies ran while one was open for 0% of the time, Pallas kernels for 0%

commit v1 on v0

--- a/solution.py
+++ b/solution.py
@@ -9,6 +9,13 @@
 LAYERS = 2
 neg_big = -1e30
 scale_dot = 0.125
+
+
+def swapped_in(x, axis, d):
+    size = lax.axis_size(axis)
+    tiles = jnp.stack([x for _ in range(size)])
+    tiles = lax.all_to_all(tiles, axis, split_axis=0, concat_axis=0)
+    return jnp.concatenate(tiles, axis=d)
 
 
 def joined(x, axis, combine):
@@ -186,7 +193,7 @@
         preferred_element_type=jnp.float32,
     )
     grad_att = grad_att.astype(jnp.bfloat16).reshape(pat_dev, lat_dev, model_width)
-    grad_all = lax.all_gather(grad_att, "contacts", axis=1, tiled=True)
+    grad_all = swapped_in(grad_att, "contacts", 1)
     delta_row = jnp.sum(
         split_heads(grad_all.astype(jnp.float32), head_count)
         * split_heads(attended_all.astype(jnp.float32), head_count),

time: 1140 us -> 1110 us (0.974)
  waiting for transfers between devices: 662 us -> 619 us
    all_gather x1 -> x0, waiting for transfers between devices: 69 us -> none  [local(): grad_all = lax.all_gather(grad_att, 'contacts', axis=1, tiled=True)]
    all_to_all x0 -> x1, waiting for transfers between devices: none -> 25.2 us  [swapped_in(): tiles = lax.all_to_all(tiles, axis, split_axis=0, concat_axis=0)]
where the time goes in v1:
time: 1110 us; the launch traced here: 1100 us
  waiting for transfers between devices  619 us (56%)
  local copies, waits for them, and re-layouts  194 us (17%)
  other arithmetic  142 us (13%)
  blocking collectives  77.1 us (7%)
  starting transfers between devices  28.2 us (3%)
  matrix products  27.9 us (3%)
  between operations  14.1 us (1%)
    all_gather x3, waiting for transfers between devices, joined(): everything = jax.tree.map(lambda part: lax.all_gather(part, axis), x)  585 us
    dynamic_slice x62, local copies, waits for them, and re-layouts, step(): return combine(so_far, jax.tree.map(lambda part: part[k], everything))  156 us
    add x31, other arithmetic, combine_parts(): split_heads(acc_a, head_count) * fac_a[..., None]  100 us
    psum x1, blocking collectives, local(): lax.psum((dq_sum * scale_dot).reshape(lat_rows, model_width), ('contacts'...  77.1 us
    all_to_all x1, waiting for transfers between devices, swapped_in(): tiles = lax.all_to_all(tiles, axis, split_axis=0, concat_axis=0)  25.2 us
    add x31, other arithmetic, combine_parts(): sum_a * fac_a + sum_b * fac_b  25.1 us
  transfers between devices with their start and end apart: 12, of which 8 were waited for; matrix products, arithmetic and copies ran while one was open for 0% of the time, Pallas kernels for 0%

profile of v1, /device:TPU:1, one launch (start us, length us, event | category | flops | bytes accessed | tf_op | source)
XLA Modules:
  0.0 1102.4 jit_solution(16979741276371553746)
XLA Ops:
  9.6 3.9 gather_fusion
  15.5 4.0 reshape.153
  19.5 5.5 copy.78
  25.4 12.2 %while.46 = (s32[]{:T(128)}, f32[2,2,256,8]{2,3,1,0:T(8,128)S(1)}, f32[2,2,256,8]{2,3,1,0:T(8,128)S(1)}, f32[2,2,256,512]{3,2,1,0:T(8,128)}, bf16[2,2,256,2,8,64...) while((s32[]{:T(128)}, f32[2,2,256,8]{2,3,1,0:T(8,128)S(1)}, ...), condition=%wide.region_3.4_spmd.clone, body=%wide.region_0.3_spmd.clone.sunk | while | flops 277864704 | bytes 21349984 | solution.py:150
  39.8 73.7 %all-gather.6.cloned.1.call-done = f32[32,4,256,8]{2,3,1,0:T(8,128)} async-done(((f32[1,4,256,8]{2,3,1,0:T(8,128)}), f32[32,4,256,8]{2,3,1,0:T(8,128)}) %all-gather.6.cloned.1.call-update) | async-done | bytes 1048592 | tf_op jit(solution)/shard_map/all_gather | solution.py:22
  114.3 76.3 %all-gather.4.cloned.1.call-done = f32[32,4,256,8]{2,3,1,0:T(8,128)} async-done(((f32[1,4,256,8]{2,3,1,0:T(8,128)}), f32[32,4,256,8]{2,3,1,0:T(8,128)}) %all-gather.4.cloned.1.call-update) | async-done | bytes 1048592 | tf_op jit(solution)/shard_map/all_gather | solution.py:22
  191.3 434.8 %all-gather.8.cloned.1.call-done = f32[32,4,256,512]{3,2,1,0:T(8,128)} async-done(((f32[1,4,256,512]{3,2,1,0:T(8,128)}), f32[32,4,256,512]{3,2,1,0:T(8,128)}) %all-gather.8.cloned.1.call-update) | async-done | bytes 67108880 | tf_op jit(solution)/shard_map/all_gather | solution.py:22
  629.7 281.9 %while.45 = (s32[]{:T(128)}, f32[4,256,8]{1,2,0:T(8,128)S(1)}, f32[4,256,8]{1,2,0:T(8,128)S(1)}, f32[4,256,512]{1,2,0:T(8,128)}, f32[32,4,256,8]{2,3,1,0:T(8,128...) while((s32[]{:T(128)}, f32[4,256,8]{1,2,0:T(8,128)S(1)}, ...), condition=%wide.region_5.6_spmd, body=%wide.region_4.5_spmd.sunk | while | flops 1622021 | bytes 15007895 | solution.py:28
  635.5 3.2 fusion.147
  644.6 3.2 fusion.147
  653.7 3.2 fusion.147
  662.8 3.2 fusion.147
  681.0 3.2 fusion.147
  690.1 3.2 fusion.147
  914.0 4.5 collective-permute-start
  935.3 3.6 collective-permute-start.5
  942.4 4.2 collective-permute-start.7
  950.6 5.7 all-to-all-start
  958.8 25.2 %all-to-all-done = bf16[32,4,8,512]{3,2,1,0:T(8,128)(2,1)} async-done(((bf16[32,4,8,512]{3,2,1,0:T(8,128)(2,1)}), bf16[32,4,8,512]{3,2,1,0:T(8,128)(2,1)}, u32[]{:S(2)}, u32[]{:S(2)}) %all-to-all-start) | async-done | bytes 1048608 | tf_op jit(solution)/shard_map/all_to_all | solution.py:17
  988.9 4.6 multiply_reduce_fusion
  993.8 22.6 %while.47 = (s32[]{:T(128)}, f32[256,8,64]{0,2,1:T(8,128)}, bf16[2,2,256,2,8,64]{2,5,1,4,3,0:T(8,128)(2,1)}, bf16[256,8,64]{0,2,1:T(8,128)(2,1)S(1)}, f32[2,2,25...) while((s32[]{:T(128)}, f32[256,8,64]{0,2,1:T(8,128)}, ...), condition=%wide.region_8.9_spmd.clone, body=%wide.region_7.8_spmd.clone.sunk | while | flops 411304192 | bytes 16205195 | solution.py:227
  999.9 5.2 fusion.155
  1011.1 5.3 fusion.155
  1017.6 77.1 %all-reduce.1 = bf16[256,512]{0,1:T(8,128)(2,1)S(1)} all-reduce(f32[256,512]{0,1:T(8,128)S(1)} %bitcast.324), channel_id=1, replica_groups=mesh['contacts'=32,'tm'=8] {'contacts','tm'}, use_global_device_ids=true, to_apply=%region_9.10 | all-reduce | flops 131072 | bytes 786432 | tf_op jit(solution)/shard_map/psum | solution.py:238
  (236 shorter events, 334.8 us)
Async XLA Ops:
  7.2 7.0 copy-start
  7.2 6.5 copy-start.7
  7.2 106.3 %all-gather.6.cloned.1.call-start = ((), (), s32[]{:S(2)}) async-start(), calls=%async_computation.2 | async-start | bytes 1081344 | tf_op jit(solution)/shard_map/all_gather | solution.py:22
  19.5 5.5 copy-start.2
  19.5 5.5 copy-start.6
  37.6 0.6 copy-start.9
  37.6 0.7 copy-start.8
  38.3 152.3 %all-gather.4.cloned.1.call-start = ((), (), s32[]{:S(2)}) async-start(), calls=%async_computation.1 | async-start | bytes 1081344 | tf_op jit(solution)/shard_map/all_gather | solution.py:22
  39.0 587.0 %all-gather.8.cloned.1.call-start = ((), (), s32[]{:S(2)}) async-start(), calls=%async_computation.3 | async-start | bytes 69206016 | tf_op jit(solution)/shard_map/all_gather | solution.py:22
  911.6 2.2 copy-start.4
  911.6 8.9 copy-start.10
  913.4 18.9 %copy-start.11 = (bf16[4,8,512]{2,1,0:T(8,128)(2,1)S(1)}, bf16[4,8,512]{2,1,0:T(8,128)(2,1)}, u32[]{:S(2)}) copy-start(bf16[4,8,512]{2,1,0:T(8,128)(2,1)} %param.29) | copy-start | bytes 98308
  913.8 18.5 %copy-start.5 = (bf16[2,3,512,512]{3,2,1,0:T(8,128)(2,1)S(1)}, bf16[2,3,512,512]{3,2,1,0:T(8,128)(2,1)}, u32[]{:S(2)}) copy-start(bf16[2,3,512,512]{3,2,1,0:T(8,128)(2,1)} %param.27) | copy-start | bytes 9437188
  914.0 6.5 collective-permute-start
  918.6 5.0 collective-permute-start.1
  925.4 4.3 collective-permute-start.2
  927.3 5.1 collective-permute-start.3
  933.4 5.6 collective-permute-start.4
  935.3 4.5 collective-permute-start.5
  940.4 6.1 collective-permute-start.6
  942.4 5.0 collective-permute-start.7
  950.6 33.3 %all-to-all-start = ((bf16[32,4,8,512]{3,2,1,0:T(8,128)(2,1)}), bf16[32,4,8,512]{3,2,1,0:T(8,128)(2,1)}, u32[]{:S(2)}, u32[]{:S(2)}) async-start(bf16[32,4,8,512]{3,2,1,0:T(8,128)(2,1)} %stack.63), calls=%async_computation | async-start | bytes 2097152 | tf_op jit(solution)/shard_map/all_to_all | solution.py:17
  993.8 100.9 %copy-start.3 = (bf16[512,512]{1,0:T(8,128)(2,1)S(1)}, bf16[512,512]{1,0:T(8,128)(2,1)}, u32[]{:S(2)}) copy-start(bf16[512,512]{1,0:T(8,128)(2,1)} %param.25) | copy-start | bytes 1572868
  1016.4 79.5 %copy-start.1 = (bf16[512,1024]{1,0:T(8,128)(2,1)S(1)}, bf16[512,1024]{1,0:T(8,128)(2,1)}, u32[]{:S(2)}) copy-start(bf16[512,1024]{1,0:T(8,128)(2,1)} %param.24) | copy-start | bytes 3145732
Sparse Core Ops, SparseCore 0:
  38.4 75.0 all-gather.5
  116.7 73.8 all-gather.3
  193.1 432.8 all-gather.7
